TPU v7x, 32 devices: a whole 2x2x4 slice. The times are simulated.
32 devices in a mesh: group: 2 (over x), expert: 16 (over z, y, core).
Axes of the slice: x: 2, y: 2, z: 4, core: 2. Of those that a mesh axis runs over, the one named last changes fastest.
Arguments:
- tokens: bfloat16 [64, 256, 1024], P(('group', 'expert')), parts along dimension 0, may hold values from -6 to 6
- w_qkv: bfloat16 [1024, 3072], P('expert'), may hold values from -0.1875 to 0.1875
- w_attn_out: bfloat16 [1024, 1024], P('expert'), may hold values from -0.1875 to 0.1875
- slot_keys: bfloat16 [1024, 32], replicated, may hold values from -0.5 to 0.5
- w_expert_in: bfloat16 [16, 1024, 2048], P('expert'), may hold values from -0.375 to 0.375
- w_expert_out: bfloat16 [16, 2048, 1024], P('expert'), may hold values from -0.125 to 0.125
Outputs:
- block_out: bfloat16 [64, 256, 1024], P(('group', 'expert')), parts along dimension 0
There are 2 independent parts, one for each index of `group`. A program takes and returns all parts, laid end to end along the dimension named above; an argument that names none is the same for every part. Nothing has to cross between parts.
All inputs are finite; a program needn't handle non-finite values.
Results may differ from a plain program's by a relative error of at most 0.009.
Values may be sent and summed in bfloat16 or wider, within the bound.
No kernel may reach another device: no remote copies, remote signals or barrier semaphores. Data moves between devices by JAX's collectives and lax.ppermute only.
A program may use at most 64 MiB of HBM per device.

v0:
```python
import math
import jax
import jax.numpy as jnp
from jax import lax
from jax.sharding import PartitionSpec as P

HEADS = 16


def layer_norm(values):
    center = values - jnp.mean(values, axis=-1, keepdims=True)
    spread = jnp.mean(center * center, axis=-1, keepdims=True)
    return center * lax.rsqrt(spread + 1e-06)


def on_device(tokens, w_qkv, w_attn_out, slot_keys, w_expert_in, w_expert_out):
    image_count, length, model_width = tokens.shape
    head_count = HEADS
    head_width = model_width // head_count
    row_count = image_count * length
    normed = (
        layer_norm(tokens.astype(jnp.float32)).astype(jnp.bfloat16).reshape(row_count, model_width)
    )
    full_qkv = lax.all_gather(w_qkv, "expert", axis=0, tiled=True)
    qkv = jnp.dot(normed, full_qkv, preferred_element_type=jnp.float32)
    packed = qkv.astype(jnp.bfloat16).reshape(image_count, length, 3, head_count, head_width)
    query = packed[:, :, 0]
    keys = packed[:, :, 1]
    values = packed[:, :, 2]
    scores = jnp.einsum(
        "bqhd,bkhd->bhqk", query, keys, preferred_element_type=jnp.float32
    ) / math.sqrt(head_width)
    weights = jax.nn.softmax(scores, axis=-1).astype(jnp.bfloat16)
    attended = jnp.einsum(
        "bhqk,bkhd->bqhd", weights, values, preferred_element_type=jnp.float32
    ).astype(jnp.bfloat16)
    attended = attended.reshape(row_count, model_width)
    full_out = lax.all_gather(w_attn_out, "expert", axis=0, tiled=True)
    projected = jnp.dot(attended, full_out, preferred_element_type=jnp.float32)
    resid = tokens.astype(jnp.float32) + projected.reshape(image_count, length, model_width)
    normed_two = layer_norm(resid).astype(jnp.bfloat16)
    slot_count = slot_keys.shape[1]
    logits = jnp.dot(
        normed_two.reshape(row_count, model_width), slot_keys, preferred_element_type=jnp.float32
    )
    logits = logits.reshape(image_count, length, slot_count)
    dispatch = jax.nn.softmax(logits, axis=1).astype(jnp.bfloat16)
    combine = jax.nn.softmax(logits, axis=2).astype(jnp.bfloat16)
    slot_inputs = jnp.einsum(
        "bsn,bsd->bnd", dispatch, normed_two, preferred_element_type=jnp.float32
    ).astype(jnp.bfloat16)
    sources = lax.axis_size("expert")
    expert_here = w_expert_in.shape[0]
    pairs = slot_count // (sources * expert_here)
    block = lax.all_to_all(slot_inputs, "expert", split_axis=1, concat_axis=1, tiled=True)
    batch = block.shape[0]
    arranged = block.reshape(batch, sources, expert_here, pairs, model_width)
    hidden = jnp.einsum(
        "bnepd,edh->bneph", arranged, w_expert_in, preferred_element_type=jnp.float32
    )
    hidden = jax.nn.gelu(hidden, approximate=False).astype(jnp.bfloat16)
    answer = jnp.einsum(
        "bneph,ehd->bnepd", hidden, w_expert_out, preferred_element_type=jnp.float32
    )
    answered = answer.astype(jnp.bfloat16).reshape(batch, slot_count, model_width)
    slot_outputs = lax.all_to_all(answered, "expert", split_axis=1, concat_axis=1, tiled=True)
    mixed = jnp.einsum("bsn,bnd->bsd", combine, slot_outputs, preferred_element_type=jnp.float32)
    return (resid + mixed).astype(jnp.bfloat16)


def solution(mesh):
    placed = (
        P(("group", "expert"), None, None),
        P("expert", None),
        P("expert", None),
        P(),
        P("expert", None, None),
        P("expert", None, None),
    )
    return jax.shard_map(
        on_device,
        mesh=mesh,
        in_specs=placed,
        out_specs=P(("group", "expert"), None, None),
        check_vma=False,
    )
```

profile of v0, /device:TPU:0, one launch (start us, length us, event | category | flops | bytes accessed | tf_op | source)
XLA Modules:
  0.0 159.9 jit_solution(4813306679087702941)
XLA Ops:
  6.5 0.0 copy-start
  6.5 0.0 copy-start.1
  6.5 0.0 all-gather.3.cloned.1.call-start
  6.5 0.7 all-gather.3.cloned.1.call-update
  7.3 0.0 all-gather.5.cloned.1.call-start
  7.3 0.7 all-gather.5.cloned.1.call-update
  8.0 1.4 convert_reduce_fusion
  9.5 0.0 copy-done.1
  9.5 0.4 fusion.14
  9.9 0.3 fusion.15
  10.2 64.0 %all-gather.3.cloned.1.call-done = bf16[1024,3072]{1,0:T(8,128)(2,1)} async-done(((bf16[64,3072]{1,0:T(8,128)(2,1)}), bf16[1024,3072]{1,0:T(8,128)(2,1)}) %all-gather.3.cloned.1.call-update) | async-done | bytes 6291472 | tf_op jit(solution)/shard_map/all_gather | solution.py:24
  74.2 7.5 %convolution_convert_fusion = bf16[512,3072]{1,0:T(8,128)(2,1)} fusion(bf16[512,1024]{1,0:T(8,128)(2,1)S(1)} %bitcast.133, bf16[1024,3072]{1,0:T(8,128)(2,1)} %all-gather.3.cloned.1.call-done), kind=kOutput, calls=%fused_computation.7 | convolution fusion | flops 3222798336 | bytes 10485760 | tf_op jit(solution)/shard_map/dot_general | solution.py:25
  81.8 8.6 %reshape.80 = bf16[2,256,3,16,64]{4,3,2,1,0:T(8,128)(2,1)} reshape(bf16[512,3072]{1,0:T(8,128)(2,1)} %convolution_convert_fusion) | data formatting | bytes 6291456 | tf_op jit(solution)/shard_map/reshape | solution.py:26
  90.4 6.0 %fusion.110 = (bf16[2,256,1,16,64]{4,3,2,1,0:T(8,128)(2,1)S(1)}, bf16[2,256,1,16,64]{4,3,2,1,0:T(8,128)(2,1)}, bf16[2,256,1,16,64]{4,3,2,1,0:T(8,128)(2,1)}) fusion(bf16[2,256,3,16,64]{4,3,2,1,0:T(8,128)(2,1)} %reshape.80), kind=kLoop, calls=%fused_computation.118 | loop fusion | bytes 6291456 | tf_op jit(solution)/shard_map/slice | solution.py:29
  96.4 3.6 %copy.48 = bf16[2,256,1,16,64]{1,4,3,0,2:T(8,128)(2,1)} copy(bf16[2,256,1,16,64]{4,3,2,1,0:T(8,128)(2,1)} %get-tuple-element.6) | data formatting | bytes 2097152
  99.9 3.5 %copy.49 = bf16[2,256,1,16,64]{1,4,3,0,2:T(8,128)(2,1)} copy(bf16[2,256,1,16,64]{4,3,2,1,0:T(8,128)(2,1)} %get-tuple-element.7) | data formatting | bytes 2097152
  103.5 2.5 %copy.47 = bf16[2,256,1,16,64]{1,4,3,0,2:T(8,128)(2,1)} copy(bf16[2,256,1,16,64]{4,3,2,1,0:T(8,128)(2,1)S(1)} %get-tuple-element.5) | data formatting | bytes 2097152
  106.0 2.8 %fusion.31 = f32[2,16,256,256]{2,3,1,0:T(8,128)S(1)} fusion(bf16[2,256,1,16,64]{1,4,3,0,2:T(8,128)(2,1)} %copy.49, bf16[2,256,1,16,64]{1,4,3,0,2:T(8,128)(2,1)} %copy.48), kind=kOutput, calls=%fused_computation.34 | convolution fusion | flops 268435456 | bytes 10485760 | tf_op jit(solution)/shard_map/bqhd,bkhd->bhqk/dot_general | solution.py:30
  108.8 0.0 copy-start.2
  108.8 6.3 %fusion.111 = (f32[2,16,256]{2,1,0:T(8,128)S(1)}, f32[2,16,256,256]{2,3,1,0:T(8,128)S(1)}) fusion(f32[2,16,256,256]{2,3,1,0:T(8,128)S(1)} %fusion.31), kind=kOutput, calls=%fused_computation.119 | output fusion | flops 8388863 | bytes 16809984 | tf_op jit(solution)/shard_map/sub | solution.py:33
  115.1 0.0 copy-done.2
  115.1 1.8 %fusion.20 = bf16[2,16,64,256]{3,2,1,0:T(8,128)(2,1)} fusion(f32[2,16,256,256]{2,3,1,0:T(8,128)S(1)} %get-tuple-element.9, f32[2,16,256]{2,1,0:T(8,128)S(1)} %get-tuple-element.8, bf16[2,256,1,16,64]{1,4,3,0,2:T(8,128)(2,1)S(1)} %copy-done.2), kind=kOutput, calls=%fused_computation.26 | convolution fusion | flops 273154048 | bytes 10518528 | tf_op jit(solution)/shard_map/bhqk,bkhd->bqhd/dot_general | solution.py:34
  117.0 0.0 all-gather.5.cloned.1.call-done
  117.0 3.3 %fusion.112 = (f32[2,256]{1,0:T(2,128)S(1)}, f32[2,256,1024]{2,1,0:T(8,128)S(1)}) fusion(bf16[2,256,1024]{1,2,0:T(8,128)(2,1)} %bitcast.134, bf16[1024,1024]{1,0:T(8,128)(2,1)} %all-gather.5.cloned.1.call-done, bf16[2,256,1024]{2,1,0:T(8,128)(2,1)S(1)} %copy-done.1), kind=kOutput, calls=%fused_computation.120 | convolution fusion | flops 1075314176 | bytes 6293504 | tf_op jit(solution)/shard_map/dot_general | solution.py:39
  120.2 0.4 multiply_reduce_fusion.1
  120.6 0.0 copy-done
  120.6 0.5 fusion.54
  121.2 0.2 fusion.113
  121.3 0.5 convolution_convert_fusion.1
  121.8 0.1 copy.37
  122.0 11.3 %all_to_all.10 = bf16[2,32,1024]{2,0,1:T(2,128)(2,1)S(1)} all-to-all(bf16[2,32,1024]{2,0,1:T(2,128)(2,1)S(1)} %copy.37), channel_id=1, replica_groups=mesh['group'=2,'expert'=16] {'expert'}, dimensions={1} | all-to-all | bytes 262144 | tf_op jit(solution)/shard_map/all_to_all | solution.py:55
  133.2 6.1 %fusion.24 = bf16[2,16,1,2,1024]{4,1,3,0,2:T(8,128)(2,1)S(1)} fusion(bf16[1,2048,1024]{2,1,0:T(8,128)(2,1)} %param.11, bf16[1,1024,2048]{2,1,0:T(8,128)(2,1)} %param.10, bf16[2,16,2,1024]{3,0,2,1:T(2,128)(2,1)S(1)} %bitcast.135), kind=kOutput, calls=%fused_computation.29 | convolution fusion | flops 545456128 | bytes 8650752 | tf_op jit(solution)/shard_map/bneph,ehd->bnepd/dot_general | solution.py:62
  139.3 0.8 copy.39
  140.1 3.5 %all-to-all-start.1 = ((bf16[2,32,1024]{2,0,1:T(2,128)(2,1)}), bf16[2,32,1024]{2,0,1:T(2,128)(2,1)S(1)}, u32[]{:S(2)}, u32[]{:S(2)}) async-start(bf16[2,32,1024]{2,0,1:T(2,128)(2,1)} %bitcast.27), calls=%async_computation.1 | async-start | bytes 262144 | tf_op jit(solution)/shard_map/all_to_all | solution.py:66
  143.7 7.9 %all-to-all-done.1 = bf16[2,32,1024]{2,0,1:T(2,128)(2,1)S(1)} async-done(((bf16[2,32,1024]{2,0,1:T(2,128)(2,1)}), bf16[2,32,1024]{2,0,1:T(2,128)(2,1)S(1)}, u32[]{:S(2)}, u32[]{:S(2)}) %all-to-all-start.1) | async-done | bytes 131104 | tf_op jit(solution)/shard_map/all_to_all | solution.py:66
  151.6 1.5 add_convert_fusion
  (5 shorter events, 0.1 us)
Async XLA Ops:
  6.5 114.1 %copy-start = (bf16[1024,32]{0,1:T(8,128)(2,1)S(1)}, bf16[1024,32]{0,1:T(8,128)(2,1)}, u32[]{:S(2)}) copy-start(bf16[1024,32]{0,1:T(8,128)(2,1)} %param.9) | copy-start | bytes 196612
  6.5 2.9 %copy-start.1 = (bf16[2,256,1024]{2,1,0:T(8,128)(2,1)S(1)}, bf16[2,256,1024]{2,1,0:T(8,128)(2,1)}, u32[]{:S(2)}) copy-start(bf16[2,256,1024]{2,1,0:T(8,128)(2,1)} %param.6) | copy-start | bytes 3145732
  6.5 67.7 %all-gather.3.cloned.1.call-start = ((), (), s32[]{:S(2)}) async-start(), calls=%async_computation.2 | async-start | bytes 6684672 | tf_op jit(solution)/shard_map/all_gather | solution.py:24
  7.3 109.7 %all-gather.5.cloned.1.call-start = ((), (), s32[]{:S(2)}) async-start(), calls=%async_computation.3 | async-start | bytes 2228224 | tf_op jit(solution)/shard_map/all_gather | solution.py:38
  108.8 6.3 %copy-start.2 = (bf16[2,256,1,16,64]{1,4,3,0,2:T(8,128)(2,1)S(1)}, bf16[2,256,1,16,64]{1,4,3,0,2:T(8,128)(2,1)}, u32[]{:S(2)}) copy-start(bf16[2,256,1,16,64]{1,4,3,0,2:T(8,128)(2,1)} %copy.47) | copy-start | bytes 3145732
  140.1 11.4 %all-to-all-start.1 = ((bf16[2,32,1024]{2,0,1:T(2,128)(2,1)}), bf16[2,32,1024]{2,0,1:T(2,128)(2,1)S(1)}, u32[]{:S(2)}, u32[]{:S(2)}) async-start(bf16[2,32,1024]{2,0,1:T(2,128)(2,1)} %bitcast.27), calls=%async_computation.1 | async-start | bytes 262144 | tf_op jit(solution)/shard_map/all_to_all | solution.py:66
Sparse Core Ops, SparseCore 0:
  9.6 64.5 all-gather.2
  76.4 39.9 all-gather.4
where the time goes:
time: 160 us
  waiting for transfers between devices  73.3 us (46%)
  local copies, waits for them, and re-layouts  25.1 us (16%)
  matrix products  24 us (15%)
  between operations  13.5 us (8%)
  blocking collectives  11.3 us (7%)
  other arithmetic  9.08 us (6%)
  starting transfers between devices  3.55 us (2%)
    all_gather x1, waiting for transfers between devices, on_device(): full_qkv = lax.all_gather(w_qkv, 'expert', axis=0, tiled=True)  64 us
    all_to_all x1, blocking collectives, on_device(): lax.all_to_all(slot_inputs, 'expert', split_axis=1, concat_axis=1, tiled=...  11.3 us
    unnamed x9, local copies, waits for them, and re-layouts  9.61 us
    reshape x1, local copies, waits for them, and re-layouts, on_device(): qkv.astype(jnp.bfloat16)  8.6 us
    all_to_all x1, waiting for transfers between devices, on_device(): lax.all_to_all(answered, 'expert', split_axis=1, concat_axis=1, tiled=True)  7.85 us
    dot_general x1, matrix products, on_device(): qkv = jnp.dot(normed, full_qkv, preferred_element_type=jnp.float32)  7.53 us
    sub x1, other arithmetic, on_device(): weights = jax.nn.softmax(scores, axis=-1).astype(jnp.bfloat16)  6.31 us
    dot_general x1, matrix products, on_device(): jnp.einsum('bneph,ehd->bnepd', hidden, w_expert_out, preferred_element_ty...  6.09 us
  transfers between devices with their start and end apart: 3, of which 2 were waited for; matrix products, arithmetic and copies ran while one was open for 28% of the time, Pallas kernels for 0%

commit v1 on v0

--- a/solution.py
+++ b/solution.py
@@ -1,3 +1,4 @@
+import functools
 import math
 import jax
 import jax.numpy as jnp
@@ -5,6 +6,30 @@
 from jax.sharding import PartitionSpec as P
 
 HEADS = 16
+
+
+def move_row(local_array, dev_axis):
+    everything = lax.axis_size(dev_axis)
+    high = lax.axis_index(dev_axis)
+    all_rows, r_now = (everything, high)
+    piece_out = local_array.shape[1] // all_rows
+    field_out = list(local_array.shape)
+    field_out[1] = piece_out
+    known = field_out[1]
+    field_out[1] = known * all_rows
+    arr_out = jnp.zeros(field_out, local_array.dtype)
+    for k0 in range(all_rows):
+        m_next = lax.dynamic_slice_in_dim(local_array, (r_now ^ k0) * piece_out, piece_out, axis=1)
+        if k0:
+            v_now = range(all_rows)
+            finding = map(lambda rr: (rr, rr ^ k0), v_now)
+            local_next = list(finding)
+            m_next = lax.ppermute(m_next, dev_axis, local_next)
+        arr_out = lax.dynamic_update_slice_in_dim(arr_out, m_next, (r_now ^ k0) * known, axis=1)
+    return arr_out
+
+
+settle_the_plate = functools.partial(move_row, dev_axis="expert")
 
 
 def layer_norm(values):
@@ -52,7 +77,7 @@
     sources = lax.axis_size("expert")
     expert_here = w_expert_in.shape[0]
     pairs = slot_count // (sources * expert_here)
-    block = lax.all_to_all(slot_inputs, "expert", split_axis=1, concat_axis=1, tiled=True)
+    block = settle_the_plate(slot_inputs)
     batch = block.shape[0]
     arranged = block.reshape(batch, sources, expert_here, pairs, model_width)
     hidden = jnp.einsum(

time: 160 us -> 175 us (1.094)
  starting transfers between devices: 3.55 us -> 25.3 us
  blocking collectives: 11.3 us -> 0 us
  waiting for transfers between devices: 73.3 us -> 76.5 us
    ppermute x0 -> x15, starting transfers between devices: none -> 21.1 us  [move_row(): m_next = lax.ppermute(m_next, dev_axis, local_next)]
    all_to_all x1 -> x0, blocking collectives: 11.3 us -> none  [on_device(): lax.all_to_all(slot_inputs, 'expert', split_axis=1, concat_axis=1, tiled=...]
    ppermute x0 -> x15, waiting for transfers between devices: none -> 3.36 us  [move_row(): m_next = lax.ppermute(m_next, dev_axis, local_next)]
  transfers between devices with their start and end apart: 3 -> 18, of which waited for: 2 -> 4; matrix products, arithmetic and copies ran while one was open for 28% -> 26% of each run, Pallas kernels for 0% -> 0%
where the time goes in v1:
time: 175 us; the launch traced here: 174 us
  waiting for transfers between devices  76.5 us (44%)
  local copies, waits for them, and re-layouts  25.5 us (15%)
  starting transfers between devices  25.3 us (14%)
  matrix products  24 us (14%)
  between operations  13.8 us (8%)
  other arithmetic  9.25 us (5%)
    all_gather x1, waiting for transfers between devices, on_device(): full_qkv = lax.all_gather(w_qkv, 'expert', axis=0, tiled=True)  63.9 us
    ppermute x15, starting transfers between devices, move_row(): m_next = lax.ppermute(m_next, dev_axis, local_next)  21.1 us
    unnamed x9, local copies, waits for them, and re-layouts  9.61 us
    reshape x1, local copies, waits for them, and re-layouts, on_device(): qkv.astype(jnp.bfloat16)  8.6 us
    all_to_all x1, waiting for transfers between devices, on_device(): lax.all_to_all(answered, 'expert', split_axis=1, concat_axis=1, tiled=True)  7.89 us
    dot_general x1, matrix products, on_device(): qkv = jnp.dot(normed, full_qkv, preferred_element_type=jnp.float32)  7.53 us
    sub x1, other arithmetic, on_device(): weights = jax.nn.softmax(scores, axis=-1).astype(jnp.bfloat16)  6.49 us
    dot_general x1, matrix products, on_device(): jnp.einsum('bneph,ehd->bnepd', hidden, w_expert_out, preferred_element_ty...  6.1 us
  transfers between devices with their start and end apart: 18, of which 4 were waited for; matrix products, arithmetic and copies ran while one was open for 26% of the time, Pallas kernels for 0%

profile of v1, /device:TPU:0, one launch (start us, length us, event | category | flops | bytes accessed | tf_op | source)
XLA Modules:
  0.0 174.4 jit_solution(3362363271507452567)
XLA Ops:
  6.5 0.0 copy-start
  6.5 0.0 all-gather.3.cloned.1.call-start
  6.5 0.7 all-gather.3.cloned.1.call-update
  7.3 0.0 all-gather.5.cloned.1.call-start
  7.3 0.7 all-gather.5.cloned.1.call-update
  8.1 1.4 convert_reduce_fusion
  9.5 0.0 copy-done.1
  9.5 0.4 fusion.14
  10.0 0.3 fusion.15
  10.4 63.9 %all-gather.3.cloned.1.call-done = bf16[1024,3072]{1,0:T(8,128)(2,1)} async-done(((bf16[64,3072]{1,0:T(8,128)(2,1)}), bf16[1024,3072]{1,0:T(8,128)(2,1)}) %all-gather.3.cloned.1.call-update) | async-done | bytes 6291472 | tf_op jit(solution)/shard_map/all_gather | solution.py:49
  74.2 7.5 %convolution_convert_fusion = bf16[512,3072]{1,0:T(8,128)(2,1)} fusion(bf16[512,1024]{1,0:T(8,128)(2,1)S(1)} %bitcast.133, bf16[1024,3072]{1,0:T(8,128)(2,1)} %all-gather.3.cloned.1.call-done), kind=kOutput, calls=%fused_computation.7 | convolution fusion | flops 3222798336 | bytes 10485760 | tf_op jit(solution)/shard_map/dot_general | solution.py:50
  81.8 8.6 %reshape.80 = bf16[2,256,3,16,64]{4,3,2,1,0:T(8,128)(2,1)} reshape(bf16[512,3072]{1,0:T(8,128)(2,1)} %convolution_convert_fusion) | data formatting | bytes 6291456 | tf_op jit(solution)/shard_map/reshape | solution.py:51
  90.4 6.0 %fusion.110 = (bf16[2,256,1,16,64]{4,3,2,1,0:T(8,128)(2,1)S(1)}, bf16[2,256,1,16,64]{4,3,2,1,0:T(8,128)(2,1)}, bf16[2,256,1,16,64]{4,3,2,1,0:T(8,128)(2,1)}) fusion(bf16[2,256,3,16,64]{4,3,2,1,0:T(8,128)(2,1)} %reshape.80), kind=kLoop, calls=%fused_computation.150 | loop fusion | bytes 6291456 | tf_op jit(solution)/shard_map/slice | solution.py:54
  96.4 3.6 %copy.69 = bf16[2,256,1,16,64]{1,4,3,0,2:T(8,128)(2,1)} copy(bf16[2,256,1,16,64]{4,3,2,1,0:T(8,128)(2,1)} %get-tuple-element.6) | data formatting | bytes 2097152
  99.9 3.5 %copy.70 = bf16[2,256,1,16,64]{1,4,3,0,2:T(8,128)(2,1)} copy(bf16[2,256,1,16,64]{4,3,2,1,0:T(8,128)(2,1)} %get-tuple-element.7) | data formatting | bytes 2097152
  103.5 2.5 %copy.68 = bf16[2,256,1,16,64]{1,4,3,0,2:T(8,128)(2,1)} copy(bf16[2,256,1,16,64]{4,3,2,1,0:T(8,128)(2,1)S(1)} %get-tuple-element.5) | data formatting | bytes 2097152
  106.0 2.8 %fusion.31 = f32[2,16,256,256]{2,3,1,0:T(8,128)S(1)} fusion(bf16[2,256,1,16,64]{1,4,3,0,2:T(8,128)(2,1)} %copy.70, bf16[2,256,1,16,64]{1,4,3,0,2:T(8,128)(2,1)} %copy.69), kind=kOutput, calls=%fused_computation.34 | convolution fusion | flops 268435456 | bytes 10485760 | tf_op jit(solution)/shard_map/bqhd,bkhd->bhqk/dot_general | solution.py:55
  108.8 0.0 copy-start.2
  108.8 6.5 %fusion.111 = (f32[2,16,256]{2,1,0:T(8,128)S(1)}, f32[2,16,256,256]{2,3,1,0:T(8,128)S(1)}) fusion(f32[2,16,256,256]{2,3,1,0:T(8,128)S(1)} %fusion.31), kind=kOutput, calls=%fused_computation.151 | output fusion | flops 8388863 | bytes 16809984 | tf_op jit(solution)/shard_map/sub | solution.py:58
  115.3 0.0 copy-done.2
  115.3 1.8 %fusion.20 = bf16[2,16,64,256]{3,2,1,0:T(8,128)(2,1)} fusion(f32[2,16,256,256]{2,3,1,0:T(8,128)S(1)} %get-tuple-element.25, f32[2,16,256]{2,1,0:T(8,128)S(1)} %get-tuple-element.24, bf16[2,256,1,16,64]{1,4,3,0,2:T(8,128)(2,1)S(1)} %copy-done.2), kind=kOutput, calls=%fused_computation.26 | convolution fusion | flops 273154048 | bytes 10518528 | tf_op jit(solution)/shard_map/bhqk,bkhd->bqhd/dot_general | solution.py:59
  117.1 3.3 %fusion.112 = (f32[2,256]{1,0:T(2,128)S(1)}, f32[2,256,1024]{2,1,0:T(8,128)S(1)}) fusion(bf16[2,256,1024]{1,2,0:T(8,128)(2,1)} %bitcast.134, bf16[1024,1024]{1,0:T(8,128)(2,1)} %all-gather.5.cloned.1.call-done, bf16[2,256,1024]{2,1,0:T(8,128)(2,1)S(1)} %copy-done.1), kind=kOutput, calls=%fused_computation.152 | convolution fusion | flops 1075314176 | bytes 6293504 | tf_op jit(solution)/shard_map/dot_general | solution.py:64
  120.4 0.4 multiply_reduce_fusion.1
  120.8 0.0 copy-done
  120.8 0.5 fusion.54
  121.3 0.2 fusion.113
  121.5 0.5 convolution_convert_fusion.1
  122.0 0.2 constant_dynamic-slice_fusion
  122.2 0.3 collective-permute-start
  122.5 0.6 collective-permute-start.1
  123.1 1.0 collective-permute-start.2
  124.1 1.5 collective-permute-start.3
  125.6 0.4 collective-permute-start.4
  126.0 0.1 broadcast_in_dim.2
  126.1 0.0 collective-permute-done
  126.1 1.5 collective-permute-start.5
  127.7 0.0 collective-permute-done.1
  127.7 1.1 collective-permute-start.6
  128.8 0.0 collective-permute-done.2
  128.8 2.2 %collective-permute-start.7 = (bf16[2,2,1024]{2,1,0:T(2,128)(2,1)S(1)}, bf16[2,2,1024]{2,1,0:T(2,128)(2,1)S(1)}, u32[]{:S(2)}, u32[]{:S(2)}) collective-permute-start(bf16[2,2,1024]{2,1,0:T(2,128)(2,1)S(1)} %get-tuple-element.15), channel_id=1, source_target_pairs={{0,8},{1,9},{2,10},{3,11},{4,12},{5,13},{6,14},{7,15},{8,0},{9,1},... | collective-permute-start | bytes 24584 | tf_op jit(solution)/shard_map/ppermute | solution.py:27
  131.1 0.0 collective-permute-done.3
  131.1 0.7 collective-permute-start.8
  131.8 0.0 collective-permute-done.4
  131.8 2.0 %collective-permute-start.9 = (bf16[2,2,1024]{2,1,0:T(2,128)(2,1)S(1)}, bf16[2,2,1024]{2,1,0:T(2,128)(2,1)S(1)}, u32[]{:S(2)}, u32[]{:S(2)}) collective-permute-start(bf16[2,2,1024]{2,1,0:T(2,128)(2,1)S(1)} %get-tuple-element.13), channel_id=1, source_target_pairs={{0,10},{1,11},{2,8},{3,9},{4,14},{5,15},{6,12},{7,13},{8,2},{9,3},... | collective-permute-start | bytes 24584 | tf_op jit(solution)/shard_map/ppermute | solution.py:27
  133.8 0.0 collective-permute-done.5
  133.8 1.5 collective-permute-start.10
  135.4 0.0 collective-permute-done.6
  135.4 2.0 %collective-permute-start.11 = (bf16[2,2,1024]{2,1,0:T(2,128)(2,1)S(1)}, bf16[2,2,1024]{2,1,0:T(2,128)(2,1)S(1)}, u32[]{:S(2)}, u32[]{:S(2)}) collective-permute-start(bf16[2,2,1024]{2,1,0:T(2,128)(2,1)S(1)} %get-tuple-element.11), channel_id=1, source_target_pairs={{0,12},{1,13},{2,14},{3,15},{4,8},{5,9},{6,10},{7,11},{8,4},{9,5},... | collective-permute-start | bytes 24584 | tf_op jit(solution)/shard_map/ppermute | solution.py:27
  137.3 0.0 collective-permute-done.7
  137.3 1.9 %collective-permute-start.12 = (bf16[2,2,1024]{2,1,0:T(2,128)(2,1)S(1)}, bf16[2,2,1024]{2,1,0:T(2,128)(2,1)S(1)}, u32[]{:S(2)}, u32[]{:S(2)}) collective-permute-start(bf16[2,2,1024]{2,1,0:T(2,128)(2,1)S(1)} %get-tuple-element.10), channel_id=1, source_target_pairs={{0,13},{1,12},{2,15},{3,14},{4,9},{5,8},{6,11},{7,10},{8,5},{9,4},... | collective-permute-start | bytes 24584 | tf_op jit(solution)/shard_map/ppermute | solution.py:27
  139.2 0.0 collective-permute-done.8
  139.2 2.0 %collective-permute-start.13 = (bf16[2,2,1024]{2,1,0:T(2,128)(2,1)S(1)}, bf16[2,2,1024]{2,1,0:T(2,128)(2,1)S(1)}, u32[]{:S(2)}, u32[]{:S(2)}) collective-permute-start(bf16[2,2,1024]{2,1,0:T(2,128)(2,1)S(1)} %get-tuple-element.9), channel_id=1, source_target_pairs={{0,14},{1,15},{2,12},{3,13},{4,10},{5,11},{6,8},{7,9},{8,6},{9,7},... | collective-permute-start | bytes 24584 | tf_op jit(solution)/shard_map/ppermute | solution.py:27
  141.3 0.0 collective-permute-done.9
  141.3 2.4 %collective-permute-start.14 = (bf16[2,2,1024]{2,1,0:T(2,128)(2,1)S(1)}, bf16[2,2,1024]{2,1,0:T(2,128)(2,1)S(1)}, u32[]{:S(2)}, u32[]{:S(2)}) collective-permute-start(bf16[2,2,1024]{2,1,0:T(2,128)(2,1)S(1)} %get-tuple-element.8), channel_id=1, source_target_pairs={{0,15},{1,14},{2,13},{3,12},{4,11},{5,10},{6,9},{7,8},{8,7},{9,6},... | collective-permute-start | bytes 24584 | tf_op jit(solution)/shard_map/ppermute | solution.py:27
  143.7 0.0 collective-permute-done.10
  143.7 0.0 collective-permute-done.11
  143.8 0.0 collective-permute-done.12
  143.8 1.8 %collective-permute-done.13 = bf16[2,2,1024]{2,1,0:T(2,128)(2,1)S(1)} collective-permute-done((bf16[2,2,1024]{2,1,0:T(2,128)(2,1)S(1)}, bf16[2,2,1024]{2,1,0:T(2,128)(2,1)S(1)}, u32[]{:S(2)}, u32[]{:S(2)}) %collective-permute-start.13) | collective-permute-done | bytes 8224 | tf_op jit(solution)/shard_map/ppermute | solution.py:27
  145.7 1.5 collective-permute-done.14
  147.2 6.1 %fusion.24 = bf16[2,16,1,2,1024]{4,1,3,0,2:T(8,128)(2,1)S(1)} fusion(bf16[1,2048,1024]{2,1,0:T(8,128)(2,1)} %param.11, bf16[1,1024,2048]{2,1,0:T(8,128)(2,1)} %param.10, bf16[2,16,2,1024]{3,0,2,1:T(2,128)(2,1)S(1)} %bitcast.135), kind=kOutput, calls=%fused_computation.29 | convolution fusion | flops 545456128 | bytes 8650752 | tf_op jit(solution)/shard_map/bneph,ehd->bnepd/dot_general | solution.py:87
  153.3 0.8 copy.60
  154.1 4.1 %all-to-all-start = ((bf16[2,32,1024]{2,0,1:T(2,128)(2,1)}), bf16[2,32,1024]{2,0,1:T(2,128)(2,1)S(1)}, u32[]{:S(2)}, u32[]{:S(2)}) async-start(bf16[2,32,1024]{2,0,1:T(2,128)(2,1)} %bitcast.27), calls=%async_computation | async-start | bytes 262144 | tf_op jit(solution)/shard_map/all_to_all | solution.py:91
  158.2 7.9 %all-to-all-done = bf16[2,32,1024]{2,0,1:T(2,128)(2,1)S(1)} async-done(((bf16[2,32,1024]{2,0,1:T(2,128)(2,1)}), bf16[2,32,1024]{2,0,1:T(2,128)(2,1)S(1)}, u32[]{:S(2)}, u32[]{:S(2)}) %all-to-all-start) | async-done | bytes 131104 | tf_op jit(solution)/shard_map/all_to_all | solution.py:91
  166.1 1.5 add_convert_fusion
  (23 shorter events, 0.3 us)
Async XLA Ops:
  6.5 114.3 %copy-start = (bf16[1024,32]{0,1:T(8,128)(2,1)S(1)}, bf16[1024,32]{0,1:T(8,128)(2,1)}, u32[]{:S(2)}) copy-start(bf16[1024,32]{0,1:T(8,128)(2,1)} %param.9) | copy-start | bytes 196612
  6.5 3.0 %copy-start.1 = (bf16[2,256,1024]{2,1,0:T(8,128)(2,1)S(1)}, bf16[2,256,1024]{2,1,0:T(8,128)(2,1)}, u32[]{:S(2)}) copy-start(bf16[2,256,1024]{2,1,0:T(8,128)(2,1)} %param.6) | copy-start | bytes 3145732
  6.5 67.7 %all-gather.3.cloned.1.call-start = ((), (), s32[]{:S(2)}) async-start(), calls=%async_computation.1 | async-start | bytes 6684672 | tf_op jit(solution)/shard_map/all_gather | solution.py:49
  7.3 109.9 %all-gather.5.cloned.1.call-start = ((), (), s32[]{:S(2)}) async-start(), calls=%async_computation.2 | async-start | bytes 2228224 | tf_op jit(solution)/shard_map/all_gather | solution.py:63
  108.8 6.5 %copy-start.2 = (bf16[2,256,1,16,64]{1,4,3,0,2:T(8,128)(2,1)S(1)}, bf16[2,256,1,16,64]{1,4,3,0,2:T(8,128)(2,1)}, u32[]{:S(2)}) copy-start(bf16[2,256,1,16,64]{1,4,3,0,2:T(8,128)(2,1)} %copy.68) | copy-start | bytes 3145732
  122.2 3.9 %collective-permute-start = (bf16[2,2,1024]{2,1,0:T(2,128)(2,1)S(1)}, bf16[2,2,1024]{2,1,0:T(2,128)(2,1)S(1)}, u32[]{:S(2)}, u32[]{:S(2)}) collective-permute-start(bf16[2,2,1024]{2,1,0:T(2,128)(2,1)S(1)} %get-tuple-element.22), channel_id=1, source_target_pairs={{0,1},{1,0},{2,3},{3,2},{4,5},{5,4},{6,7},{7,6},{8,9},{9,8},{10,11... | collective-permute-start | bytes 24584 | tf_op jit(solution)/shard_map/ppermute | solution.py:27
  122.5 5.2 %collective-permute-start.1 = (bf16[2,2,1024]{2,1,0:T(2,128)(2,1)S(1)}, bf16[2,2,1024]{2,1,0:T(2,128)(2,1)S(1)}, u32[]{:S(2)}, u32[]{:S(2)}) collective-permute-start(bf16[2,2,1024]{2,1,0:T(2,128)(2,1)S(1)} %get-tuple-element.21), channel_id=1, source_target_pairs={{0,2},{1,3},{2,0},{3,1},{4,6},{5,7},{6,4},{7,5},{8,10},{9,11},{10,... | collective-permute-start | bytes 24584 | tf_op jit(solution)/shard_map/ppermute | solution.py:27
  123.1 5.7 %collective-permute-start.2 = (bf16[2,2,1024]{2,1,0:T(2,128)(2,1)S(1)}, bf16[2,2,1024]{2,1,0:T(2,128)(2,1)S(1)}, u32[]{:S(2)}, u32[]{:S(2)}) collective-permute-start(bf16[2,2,1024]{2,1,0:T(2,128)(2,1)S(1)} %get-tuple-element.20), channel_id=1, source_target_pairs={{0,3},{1,2},{2,1},{3,0},{4,7},{5,6},{6,5},{7,4},{8,11},{9,10},{10,... | collective-permute-start | bytes 24584 | tf_op jit(solution)/shard_map/ppermute | solution.py:27
  124.1 6.9 %collective-permute-start.3 = (bf16[2,2,1024]{2,1,0:T(2,128)(2,1)S(1)}, bf16[2,2,1024]{2,1,0:T(2,128)(2,1)S(1)}, u32[]{:S(2)}, u32[]{:S(2)}) collective-permute-start(bf16[2,2,1024]{2,1,0:T(2,128)(2,1)S(1)} %get-tuple-element.19), channel_id=1, source_target_pairs={{0,4},{1,5},{2,6},{3,7},{4,0},{5,1},{6,2},{7,3},{8,12},{9,13},{10,... | collective-permute-start | bytes 24584 | tf_op jit(solution)/shard_map/ppermute | solution.py:27
  125.6 6.2 %collective-permute-start.4 = (bf16[2,2,1024]{2,1,0:T(2,128)(2,1)S(1)}, bf16[2,2,1024]{2,1,0:T(2,128)(2,1)S(1)}, u32[]{:S(2)}, u32[]{:S(2)}) collective-permute-start(bf16[2,2,1024]{2,1,0:T(2,128)(2,1)S(1)} %get-tuple-element.18), channel_id=1, source_target_pairs={{0,5},{1,4},{2,7},{3,6},{4,1},{5,0},{6,3},{7,2},{8,13},{9,12},{10,... | collective-permute-start | bytes 24584 | tf_op jit(solution)/shard_map/ppermute | solution.py:27
  126.1 7.7 %collective-permute-start.5 = (bf16[2,2,1024]{2,1,0:T(2,128)(2,1)S(1)}, bf16[2,2,1024]{2,1,0:T(2,128)(2,1)S(1)}, u32[]{:S(2)}, u32[]{:S(2)}) collective-permute-start(bf16[2,2,1024]{2,1,0:T(2,128)(2,1)S(1)} %get-tuple-element.17), channel_id=1, source_target_pairs={{0,6},{1,7},{2,4},{3,5},{4,2},{5,3},{6,0},{7,1},{8,14},{9,15},{10,... | collective-permute-start | bytes 24584 | tf_op jit(solution)/shard_map/ppermute | solution.py:27
  127.7 7.7 %collective-permute-start.6 = (bf16[2,2,1024]{2,1,0:T(2,128)(2,1)S(1)}, bf16[2,2,1024]{2,1,0:T(2,128)(2,1)S(1)}, u32[]{:S(2)}, u32[]{:S(2)}) collective-permute-start(bf16[2,2,1024]{2,1,0:T(2,128)(2,1)S(1)} %get-tuple-element.16), channel_id=1, source_target_pairs={{0,7},{1,6},{2,5},{3,4},{4,3},{5,2},{6,1},{7,0},{8,15},{9,14},{10,... | collective-permute-start | bytes 24584 | tf_op jit(solution)/shard_map/ppermute | solution.py:27
  128.8 8.5 %collective-permute-start.7 = (bf16[2,2,1024]{2,1,0:T(2,128)(2,1)S(1)}, bf16[2,2,1024]{2,1,0:T(2,128)(2,1)S(1)}, u32[]{:S(2)}, u32[]{:S(2)}) collective-permute-start(bf16[2,2,1024]{2,1,0:T(2,128)(2,1)S(1)} %get-tuple-element.15), channel_id=1, source_target_pairs={{0,8},{1,9},{2,10},{3,11},{4,12},{5,13},{6,14},{7,15},{8,0},{9,1},... | collective-permute-start | bytes 24584 | tf_op jit(solution)/shard_map/ppermute | solution.py:27
  131.1 8.1 %collective-permute-start.8 = (bf16[2,2,1024]{2,1,0:T(2,128)(2,1)S(1)}, bf16[2,2,1024]{2,1,0:T(2,128)(2,1)S(1)}, u32[]{:S(2)}, u32[]{:S(2)}) collective-permute-start(bf16[2,2,1024]{2,1,0:T(2,128)(2,1)S(1)} %get-tuple-element.14), channel_id=1, source_target_pairs={{0,9},{1,8},{2,11},{3,10},{4,13},{5,12},{6,15},{7,14},{8,1},{9,0},... | collective-permute-start | bytes 24584 | tf_op jit(solution)/shard_map/ppermute | solution.py:27
  131.8 9.5 %collective-permute-start.9 = (bf16[2,2,1024]{2,1,0:T(2,128)(2,1)S(1)}, bf16[2,2,1024]{2,1,0:T(2,128)(2,1)S(1)}, u32[]{:S(2)}, u32[]{:S(2)}) collective-permute-start(bf16[2,2,1024]{2,1,0:T(2,128)(2,1)S(1)} %get-tuple-element.13), channel_id=1, source_target_pairs={{0,10},{1,11},{2,8},{3,9},{4,14},{5,15},{6,12},{7,13},{8,2},{9,3},... | collective-permute-start | bytes 24584 | tf_op jit(solution)/shard_map/ppermute | solution.py:27
  133.8 9.9 %collective-permute-start.10 = (bf16[2,2,1024]{2,1,0:T(2,128)(2,1)S(1)}, bf16[2,2,1024]{2,1,0:T(2,128)(2,1)S(1)}, u32[]{:S(2)}, u32[]{:S(2)}) collective-permute-start(bf16[2,2,1024]{2,1,0:T(2,128)(2,1)S(1)} %get-tuple-element.12), channel_id=1, source_target_pairs={{0,11},{1,10},{2,9},{3,8},{4,15},{5,14},{6,13},{7,12},{8,3},{9,2},... | collective-permute-start | bytes 24584 | tf_op jit(solution)/shard_map/ppermute | solution.py:27
  135.4 8.4 %collective-permute-start.11 = (bf16[2,2,1024]{2,1,0:T(2,128)(2,1)S(1)}, bf16[2,2,1024]{2,1,0:T(2,128)(2,1)S(1)}, u32[]{:S(2)}, u32[]{:S(2)}) collective-permute-start(bf16[2,2,1024]{2,1,0:T(2,128)(2,1)S(1)} %get-tuple-element.11), channel_id=1, source_target_pairs={{0,12},{1,13},{2,14},{3,15},{4,8},{5,9},{6,10},{7,11},{8,4},{9,5},... | collective-permute-start | bytes 24584 | tf_op jit(solution)/shard_map/ppermute | solution.py:27
  137.3 6.4 %collective-permute-start.12 = (bf16[2,2,1024]{2,1,0:T(2,128)(2,1)S(1)}, bf16[2,2,1024]{2,1,0:T(2,128)(2,1)S(1)}, u32[]{:S(2)}, u32[]{:S(2)}) collective-permute-start(bf16[2,2,1024]{2,1,0:T(2,128)(2,1)S(1)} %get-tuple-element.10), channel_id=1, source_target_pairs={{0,13},{1,12},{2,15},{3,14},{4,9},{5,8},{6,11},{7,10},{8,5},{9,4},... | collective-permute-start | bytes 24584 | tf_op jit(solution)/shard_map/ppermute | solution.py:27
  139.2 6.4 %collective-permute-start.13 = (bf16[2,2,1024]{2,1,0:T(2,128)(2,1)S(1)}, bf16[2,2,1024]{2,1,0:T(2,128)(2,1)S(1)}, u32[]{:S(2)}, u32[]{:S(2)}) collective-permute-start(bf16[2,2,1024]{2,1,0:T(2,128)(2,1)S(1)} %get-tuple-element.9), channel_id=1, source_target_pairs={{0,14},{1,15},{2,12},{3,13},{4,10},{5,11},{6,8},{7,9},{8,6},{9,7},... | collective-permute-start | bytes 24584 | tf_op jit(solution)/shard_map/ppermute | solution.py:27
  141.3 5.8 %collective-permute-start.14 = (bf16[2,2,1024]{2,1,0:T(2,128)(2,1)S(1)}, bf16[2,2,1024]{2,1,0:T(2,128)(2,1)S(1)}, u32[]{:S(2)}, u32[]{:S(2)}) collective-permute-start(bf16[2,2,1024]{2,1,0:T(2,128)(2,1)S(1)} %get-tuple-element.8), channel_id=1, source_target_pairs={{0,15},{1,14},{2,13},{3,12},{4,11},{5,10},{6,9},{7,8},{8,7},{9,6},... | collective-permute-start | bytes 24584 | tf_op jit(solution)/shard_map/ppermute | solution.py:27
  154.1 12.1 %all-to-all-start = ((bf16[2,32,1024]{2,0,1:T(2,128)(2,1)}), bf16[2,32,1024]{2,0,1:T(2,128)(2,1)S(1)}, u32[]{:S(2)}, u32[]{:S(2)}) async-start(bf16[2,32,1024]{2,0,1:T(2,128)(2,1)} %bitcast.27), calls=%async_computation | async-start | bytes 262144 | tf_op jit(solution)/shard_map/all_to_all | solution.py:91
Sparse Core Ops, SparseCore 0:
  9.6 64.5 all-gather.2
  76.4 39.9 all-gather.4
